TPU v7x, 256 devices: a whole 4x4x8 slice. The times are simulated.
256 devices in a mesh: aux: 8 (over x_lo, y), occ: 32 (over x_hi, z, core).
Axes of the slice: x: 4 (x_hi: 2, x_lo: 2; x = x_hi * 2 + x_lo), y: 4, z: 8, core: 2. Of those that a mesh axis runs over, the one named last changes fastest.
Arguments:
- factor: bfloat16 [6144, 32, 1536], P('aux', 'occ'), may hold values from -0.67578125 to 0.67578125
- occ_energy: float32 [1024], replicated, may hold values from -3 to -0.5
- vir_energy: float32 [3072], replicated, may hold values from 0.5 to 4
- occ_pick: int32 [32], replicated, may hold values from 0 to 1023
- vir_pick: int32 [1536], replicated, may hold values from 0 to 3071
Outputs:
- gamma: float32 [6144, 32, 1536], P('aux', 'occ')
All inputs are finite; a program needn't handle non-finite values.
Results may differ from a plain program's by a relative error of at most 0.0024.
Values may be sent and summed in bfloat16 or wider, within the bound.
A program may use at most 192 MiB of HBM per device.

v0:
```python
import jax
import jax.numpy as jnp
from jax import lax
from jax.sharding import PartitionSpec as P


def shifted(block, axis, distance):
    devices = range(lax.axis_size(axis))
    route = [((i - distance) % len(devices), i) for i in devices]
    return lax.ppermute(block, axis, route)


def pair_density(left_block, right_block, pair_level, vir_levels, vir_rows):
    integrals = lax.psum_scatter(
        lax.dot_general(
            right_block, left_block, (((0,), (0,)), ((), ())), preferred_element_type=jnp.float32
        ),
        "aux",
        scatter_dimension=0,
        tiled=True,
    )
    divisor = pair_level - vir_rows[:, None] - vir_levels[None, :]
    amplitudes = (integrals / divisor).astype(jnp.bfloat16)
    return jnp.dot(
        right_block,
        lax.all_gather(amplitudes, "aux", axis=0, tiled=True),
        preferred_element_type=jnp.float32,
    )


def on_device(factor, occ_energy, vir_energy, occ_pick, vir_pick):
    aux_count = lax.axis_size("aux")
    occ_count = lax.axis_size("occ")
    aux_place = lax.axis_index("aux")
    occ_place = lax.axis_index("occ")
    local_occ = factor.shape[1]
    virtuals = factor.shape[2]
    row_count = virtuals // aux_count
    occ_levels = jnp.take(occ_energy, occ_pick)
    vir_levels = jnp.take(vir_energy, vir_pick)
    row_start = aux_place * row_count
    vir_rows = lax.dynamic_slice_in_dim(vir_levels, row_start, row_count)
    near_block = shifted(factor, "occ", 1)
    far_block = shifted(near_block, "occ", 1)
    partners = ((1, near_block), (2, far_block))
    left_block = factor[:, 0, :]
    own_level = lax.dynamic_index_in_dim(occ_levels, occ_place * local_occ + 0, keepdims=False)
    density = jnp.zeros((factor.shape[0], virtuals), jnp.float32)
    for distance, block in partners:
        source_base = (occ_place - distance) % occ_count * local_occ
        right_block = block[:, 0, :]
        other_level = lax.dynamic_index_in_dim(occ_levels, source_base + 0, keepdims=False)
        density = density + pair_density(
            left_block, right_block, own_level + other_level, vir_levels, vir_rows
        )
    results = [density]
    return jnp.stack(results, axis=1)


def solution(mesh):
    placed = (P("aux", "occ", None), P(), P(), P(), P())
    return jax.shard_map(
        on_device, mesh=mesh, in_specs=placed, out_specs=P("aux", "occ", None), check_vma=False
    )
```

profile of v0, /device:TPU:2, one launch (start us, length us, event | category | flops | bytes accessed | tf_op | source)
XLA Modules:
  0.0 425.6 jit_solution(7457580632704250876)
XLA Ops:
  6.5 0.0 copy-start
  6.5 0.0 reduce-scatter.3.cloned.1.call-start
  6.5 0.0 collective-permute-start
  6.5 33.6 %collective-permute-done = bf16[768,1,1536]{2,0,1:T(8,128)(2,1)S(1)} collective-permute-done((bf16[768,1,1536]{2,0,1:T(8,128)(2,1)}, bf16[768,1,1536]{2,0,1:T(8,128)(2,1)S(1)}, u32[]{:S(2)}, u32[]{:S(2)}) %collective-permute-start) | collective-permute-done | bytes 2359328 | tf_op jit(solution)/shard_map/ppermute | solution.py:10
  40.1 0.0 copy-start.4
  40.1 1.4 copy-done.4
  41.5 7.9 %fusion.4 = f32[1536,1536]{1,0:T(8,128)} fusion(bf16[768,1,1536]{2,0,1:T(8,128)(2,1)} %param.5, bf16[768,1,1536]{2,0,1:T(8,128)(2,1)S(1)} %collective-permute-done), kind=kOutput, calls=%fused_computation.7 | convolution fusion | flops 3623878656 | bytes 14155776 | tf_op jit(solution)/shard_map/dot_general | solution.py:15
  49.5 0.0 copy-start.3
  49.5 0.0 reduce-scatter.3.cloned.1.call-update
  49.5 0.0 reduce-scatter.5.cloned.1.call-start
  49.6 0.1 collective-permute-start.1
  49.7 32.2 %collective-permute-done.1 = bf16[768,1,1536]{2,0,1:T(8,128)(2,1)S(1)} collective-permute-done((bf16[768,1,1536]{2,0,1:T(8,128)(2,1)}, bf16[768,1,1536]{2,0,1:T(8,128)(2,1)S(1)}, u32[]{:S(2)}, u32[]{:S(2)}) %collective-permute-start.1) | collective-permute-done | bytes 2359328 | tf_op jit(solution)/shard_map/ppermute | solution.py:10
  81.8 0.0 copy-start.6
  81.8 1.4 copy-done.6
  83.2 0.0 copy-done.3
  83.2 6.3 %fusion.1 = f32[1536,1536]{1,0:T(8,128)} fusion(bf16[768,1,1536]{2,0,1:T(8,128)(2,1)S(1)} %collective-permute-done.1, bf16[768,1,1536]{2,0,1:T(8,128)(2,1)S(1)} %copy-done.3), kind=kOutput, calls=%fused_computation.4 | convolution fusion | flops 3623878656 | bytes 14155776 | tf_op jit(solution)/shard_map/dot_general | solution.py:15
  89.5 0.0 copy-start.7
  89.5 0.0 copy-start.1
  89.5 0.0 copy-start.2
  89.6 0.0 reduce-scatter.5.cloned.1.call-update
  89.6 0.0 all-gather.3.cloned.1.call-start
  89.7 0.5 copy-done.7
  90.2 0.0 copy-done.1
  90.2 0.7 gather_fusion
  90.9 0.7 fusion.9
  94.3 0.0 copy-done.2
  94.3 0.0 copy-done
  94.3 8.4 %gather_fusion.1 = f32[1536]{0:T(1024)S(1)} fusion(f32[3072]{0:T(1024)S(1)} %copy-done, s32[2048]{0:T(1024)S(1)} %pad_clamp_fusion), kind=kCustom, calls=%fused_computation.1 | custom fusion | bytes 18432 | tf_op jit(solution)/shard_map/jit(_take)/gather | solution.py:40
  102.7 0.1 dynamic-slice_subtract_fusion
  102.8 69.8 %reduce-scatter.3.cloned.1.call-done = f32[192,1536]{1,0:T(8,128)} async-done(((f32[1536,1536]{1,0:T(8,128)}), f32[192,1536]{1,0:T(8,128)}) %reduce-scatter.3.cloned.1.call-update) | async-done | bytes 1179664 | tf_op jit(solution)/shard_map/reduce_scatter | solution.py:14
  172.6 101.1 %reduce-scatter.5.cloned.1.call-done = f32[192,1536]{1,0:T(8,128)} async-done(((f32[1536,1536]{1,0:T(8,128)}), f32[192,1536]{1,0:T(8,128)}) %reduce-scatter.5.cloned.1.call-update) | async-done | bytes 1179664 | tf_op jit(solution)/shard_map/reduce_scatter | solution.py:14
  273.7 0.0 copy-start.5
  273.7 3.2 divide_convert_fusion
  276.9 0.0 all-gather.3.cloned.1.call-update
  276.9 0.2 all-gather.5.cloned.1.call-start
  277.1 0.3 all-gather.5.cloned.1.call-update
  277.5 58.5 %all-gather.3.cloned.1.call-done = bf16[1536,1536]{1,0:T(8,128)(2,1)} async-done(((bf16[192,1536]{1,0:T(8,128)(2,1)}), bf16[1536,1536]{1,0:T(8,128)(2,1)}) %all-gather.3.cloned.1.call-update) | async-done | bytes 4718608 | tf_op jit(solution)/shard_map/all_gather | solution.py:26
  336.0 0.0 copy-done.5
  336.0 8.4 %fusion.6 = f32[1536,768]{1,0:T(8,128)} fusion(bf16[1536,1536]{1,0:T(8,128)(2,1)} %all-gather.3.cloned.1.call-done, bf16[768,1,1536]{2,0,1:T(8,128)(2,1)S(1)} %copy-done.5), kind=kOutput, calls=%fused_computation.9 | convolution fusion | flops 3623878656 | bytes 11796480 | tf_op jit(solution)/shard_map/dot_general | solution.py:24
  344.4 52.1 %all-gather.5.cloned.1.call-done = bf16[1536,1536]{1,0:T(8,128)(2,1)} async-done(((bf16[192,1536]{1,0:T(8,128)(2,1)}), bf16[1536,1536]{1,0:T(8,128)(2,1)}) %all-gather.5.cloned.1.call-update) | async-done | bytes 4718608 | tf_op jit(solution)/shard_map/all_gather | solution.py:26
  396.5 10.5 %add_bitcast_fusion = f32[768,1,1536]{0,2,1:T(8,128)} fusion(f32[1536,768]{1,0:T(8,128)} %fusion.6, bf16[1536,1536]{1,0:T(8,128)(2,1)} %all-gather.5.cloned.1.call-done, bf16[768,1,1536]{2,0,1:T(8,128)(2,1)} %copy-done.6), kind=kOutput, calls=%fused_computation.2 | convolution fusion | flops 3625058304 | bytes 16515072 | tf_op jit(solution)/shard_map/dot_general | solution.py:24
  407.0 12.1 %copy.7 = f32[768,1,1536]{2,1,0:T(1,128)} copy(f32[768,1,1536]{0,2,1:T(8,128)} %add_bitcast_fusion) | data formatting | bytes 9437184 | tf_op jit(solution)/shard_map/stack | solution.py:57
  (6 shorter events, 0.0 us)
Async XLA Ops:
  6.5 87.8 %copy-start = (f32[3072]{0:T(1024)S(1)}, f32[3072]{0:T(1024)}, u32[]{:S(2)}) copy-start(f32[3072]{0:T(1024)} %param.7) | copy-start | bytes 36868
  6.5 166.1 %reduce-scatter.3.cloned.1.call-start = ((), (), s32[]{:S(2)}) async-start(), calls=%async_computation.2 | async-start | bytes 10616832 | tf_op jit(solution)/shard_map/reduce_scatter | solution.py:14
  6.5 33.6 %collective-permute-start = (bf16[768,1,1536]{2,0,1:T(8,128)(2,1)}, bf16[768,1,1536]{2,0,1:T(8,128)(2,1)S(1)}, u32[]{:S(2)}, u32[]{:S(2)}) collective-permute-start(bf16[768,1,1536]{2,0,1:T(8,128)(2,1)} %param.5), channel_id=1, source_target_pairs={{31,0},{0,1},{1,2},{2,3},{3,4},{4,5},{5,6},{6,7},{7,8},{8,9},{9,10... | collective-permute-start | bytes 7077896 | tf_op jit(solution)/shard_map/ppermute | solution.py:10
  40.1 1.4 copy-start.4
  49.5 33.8 %copy-start.3 = (bf16[768,1,1536]{2,0,1:T(8,128)(2,1)S(1)}, bf16[768,1,1536]{2,0,1:T(8,128)(2,1)}, u32[]{:S(2)}) copy-start(bf16[768,1,1536]{2,0,1:T(8,128)(2,1)} %param.5) | copy-start | bytes 7077892
  49.5 224.2 %reduce-scatter.5.cloned.1.call-start = ((), (), s32[]{:S(2)}) async-start(), calls=%async_computation.4 | async-start | bytes 10616832 | tf_op jit(solution)/shard_map/reduce_scatter | solution.py:14
  49.6 32.3 %collective-permute-start.1 = (bf16[768,1,1536]{2,0,1:T(8,128)(2,1)}, bf16[768,1,1536]{2,0,1:T(8,128)(2,1)S(1)}, u32[]{:S(2)}, u32[]{:S(2)}) collective-permute-start(bf16[768,1,1536]{2,0,1:T(8,128)(2,1)} %copy-done.4), channel_id=1, source_target_pairs={{31,0},{0,1},{1,2},{2,3},{3,4},{4,5},{5,6},{6,7},{7,8},{8,9},{9,10... | collective-permute-start | bytes 7077896 | tf_op jit(solution)/shard_map/ppermute | solution.py:10
  81.8 1.4 copy-start.6
  89.5 0.7 copy-start.7
  89.5 0.7 copy-start.1
  89.5 4.7 %copy-start.2 = (s32[1536]{0:T(1024)S(1)}, s32[1536]{0:T(1024)}, u32[]{:S(2)}) copy-start(s32[1536]{0:T(1024)} %param.9) | copy-start | bytes 18436
  89.6 246.4 %all-gather.3.cloned.1.call-start = ((), (), s32[]{:S(2)}) async-start(), calls=%async_computation.3 | async-start | bytes 5308416 | tf_op jit(solution)/shard_map/all_gather | solution.py:26
  273.7 62.3 %copy-start.5 = (bf16[768,1,1536]{2,0,1:T(8,128)(2,1)S(1)}, bf16[768,1,1536]{2,0,1:T(8,128)(2,1)}, u32[]{:S(2)}) copy-start(bf16[768,1,1536]{2,0,1:T(8,128)(2,1)} %copy-done.4) | copy-start | bytes 7077892
  276.9 119.6 %all-gather.5.cloned.1.call-start = ((), (), s32[]{:S(2)}) async-start(), calls=%async_computation.5 | async-start | bytes 5308416 | tf_op jit(solution)/shard_map/all_gather | solution.py:26
Sparse Core Ops, SparseCore 0:
  49.6 122.9 reduce-scatter.2
  175.2 98.4 reduce-scatter.4
  277.0 58.8 all-gather.2
  337.6 58.8 all-gather.4
where the time goes:
time: 428 us; the launch traced here: 426 us
  waiting for transfers between devices  348 us (81%)
  matrix products  33.2 us (8%)
  local copies, waits for them, and re-layouts  25.2 us (6%)
  between operations  15.9 us (4%)
    reduce_scatter x2, waiting for transfers between devices, pair_density(): lax.psum_scatter(lax.dot_general(right_block, left_block, (((0,), (0,)),...  171 us
    all_gather x2, waiting for transfers between devices, pair_density(): lax.all_gather(amplitudes, 'aux', axis=0, tiled=True)  111 us
    ppermute x2, waiting for transfers between devices, shifted(): return lax.ppermute(block, axis, route)  65.8 us
    dot_general x2, matrix products, pair_density(): jnp.dot(right_block, lax.all_gather(amplitudes, 'aux', axis=0, tiled=True...  18.9 us
    dot_general x2, matrix products, pair_density(): lax.dot_general(right_block, left_block, (((0,), (0,)), ((), ())), prefer...  14.3 us
    another operation x1, local copies, waits for them, and re-layouts, on_device(): return jnp.stack(results, axis=1)  12.1 us
  transfers between devices with their start and end apart: 6, of which 6 were waited for; matrix products, arithmetic and copies ran while one was open for 6% of the time, Pallas kernels for 0%

commit v1 on v0

v1 whole, which is shorter than its diff:
```python
import functools

import jax
import jax.numpy as jnp
from jax import lax
from jax.experimental import pallas as pl
from jax.experimental.pallas import tpu as pltpu
from jax.sharding import PartitionSpec as P

MESH = pl.DeviceIdType.MESH
LANES = 128


def kernel(
    n_y, n_occ, f_ref, oe_ref, ve_ref, op_ref, vp_ref, out_ref,
    fx, ft, jj, jx, sb, rb, acc, tt, g1, vcol, vrow,
    g_s, g_r, z_s, z_r, s_s, s_r, rs_s, rs_r, ax_s, ax_r, a1_s, a1_r, a2_s, a2_r,
):
    rows, virt = f_ref.shape
    half = virt // 2
    chunk = virt // n_y
    sub = chunk // 2
    aux, occ = lax.axis_index("aux"), lax.axis_index("occ")
    h, y = aux // n_y, aux % n_y
    core = occ % 2

    def at_y(step):
        return {"aux": h * n_y + (y + step) % n_y}

    partner = {"aux": (1 - h) * n_y + y}
    sibling = {"occ": occ + 1 - 2 * core}
    ahead = {"occ": (occ + 2) % n_occ}
    behind = {"occ": (occ + n_occ - 2) % n_occ}

    def send(src, dst, s_sem, r_sem, where):
        return pltpu.make_async_remote_copy(
            src_ref=src, dst_ref=dst, send_sem=s_sem, recv_sem=r_sem,
            device_id=where, device_id_type=MESH,
        )

    def cols(start, size):
        return pl.ds(pl.multiple_of(start, LANES), size)

    mine, other = cols(h * half, half), cols((1 - h) * half, half)

    barrier = pltpu.get_barrier_semaphore()
    peers = [partner, sibling, ahead, behind] + [at_y(k) for k in range(1, n_y)]
    for peer in peers:
        pl.semaphore_signal(barrier, inc=1, device_id=peer, device_id_type=MESH)
    pl.semaphore_wait(barrier, len(peers))

    def gather(k, half_at):
        c = cols((half_at * (n_y // 2) + k) % n_y * chunk, chunk)
        return send(f_ref.at[:, c], fx.at[:, c], g_s.at[k], g_r.at[k], partner)

    for k in range(n_y):
        gather(k, 1 - h).start()

    ahead_parts = (
        send(f_ref.at[:, mine], jj.at[1, :, mine], z_s.at[0], z_r.at[0], ahead),
        send(fx.at[:, mine], jx.at[1], z_s.at[1], z_r.at[1], ahead),
        send(f_ref.at[:, other], jj.at[1, :, other], z_s.at[2], z_r.at[2], ahead),
    )
    down_parts = (
        send(f_ref.at[:, mine], jj.at[0, :, mine], s_s.at[0], s_r.at[0], sibling),
        send(fx.at[:, mine], jx.at[0], s_s.at[1], s_r.at[1], sibling),
        send(f_ref.at[:, other], jj.at[0, :, other], s_s.at[2], s_r.at[2], sibling),
    )
    up_parts = (
        send(jj.at[1, :, mine], jj.at[0, :, mine], s_s.at[0], s_r.at[0], sibling),
        send(jx.at[1], jx.at[0], s_s.at[1], s_r.at[1], sibling),
        send(jj.at[1, :, other], jj.at[0, :, other], s_s.at[2], s_r.at[2], sibling),
    )
    ahead_parts[0].start()

    @pl.when(core == 0)
    def _():
        down_parts[0].start()

    def turn(src, c, at):
        def body(t, carry):
            start = pl.multiple_of(c * chunk + t * LANES, LANES)
            ft[pl.ds(start, LANES), at * rows : (at + 1) * rows] = src[:, pl.ds(start, LANES)].T
            return carry

        lax.fori_loop(0, chunk // LANES, body, 0)

    def turn_own(k, carry):
        turn(f_ref, (h * (n_y // 2) + k) % n_y, 0)
        return carry

    lax.fori_loop(0, n_y, turn_own, 0)

    n_tiles = ve_ref.shape[0]
    lane = lax.broadcasted_iota(jnp.int32, (LANES, LANES), 1)

    def levels(g, carry):
        pick = jnp.broadcast_to(vp_ref[pl.ds(g, 1), :], (LANES, LANES)).T

        def one(m, total):
            energy = jnp.broadcast_to(ve_ref[pl.ds(m, 1), :], (LANES, LANES))
            return total + jnp.where(pick == lane + m * LANES, energy, 0.0)

        total = lax.fori_loop(0, n_tiles, one, jnp.zeros((LANES, LANES), jnp.float32))
        level = jnp.broadcast_to(jnp.sum(total, axis=1, keepdims=True), (LANES, LANES))
        start = pl.multiple_of(g * LANES, LANES)
        vcol[pl.ds(start, LANES), :] = level
        vrow[:, pl.ds(start, LANES)] = level.T[:8]
        return carry

    lax.fori_loop(0, virt // LANES, levels, 0)

    spot = lax.broadcasted_iota(jnp.int32, oe_ref.shape, 0) * LANES
    spot = spot + lax.broadcasted_iota(jnp.int32, oe_ref.shape, 1)

    def occ_level(orbital):
        found = jnp.where(spot == op_ref[orbital], oe_ref[...], 0.0)
        return jnp.sum(jnp.sum(found, axis=1, keepdims=True), axis=0, keepdims=True)

    def own_chunk(k):
        return (h * (n_y // 2) + k) % n_y

    def arrived(k):
        gather(k, h).wait_recv()
        turn(fx, own_chunk(k), 1)

    for k in range(n_y // 2):
        gather(k, h).wait_recv()
    ahead_parts[1].start()

    @pl.when(core == 0)
    def _():
        down_parts[1].start()
        down_parts[2].start()

    ahead_parts[2].start()
    for k in range(n_y // 2):
        turn(fx, own_chunk(k), 1)

    width = 256

    def partial_integrals(s, c):
        r = (c + n_y - y) % n_y
        a_rows = pl.ds(pl.multiple_of(c * chunk, chunk), chunk)

        def body(t, carry):
            start = pl.multiple_of(t * width, width)
            b_cols = cols(h * half + start, width)
            total = jnp.dot(
                ft[a_rows, :rows], jj[s, :, b_cols], preferred_element_type=jnp.float32
            )
            total = total + jnp.dot(
                ft[a_rows, rows:], jx[s, :, pl.ds(start, width)],
                preferred_element_type=jnp.float32,
            )

            @pl.when(r == 0)
            def _():
                acc[s, :, pl.ds(start, width)] = total

            @pl.when(r != 0)
            def _():
                sb[s, r - 1, :, pl.ds(start, width)] = total.astype(jnp.bfloat16)

            return carry

        lax.fori_loop(0, half // width, body, 0)

        @pl.when(r != 0)
        def _():
            send(
                sb.at[s, r - 1], rb.at[s, n_y - 1 - r], rs_s.at[s, r - 1],
                rs_r.at[s, n_y - 1 - r], {"aux": h * n_y + c},
            ).start()

    my_rows = pl.ds(pl.multiple_of(y * chunk, chunk), chunk)

    def finish(s):
        for k in range(n_y - 1):
            send(
                sb.at[s, k], rb.at[s, k], rs_s.at[s, k], rs_r.at[s, k], at_y(1)
            ).wait_recv()
        level = occ_level(occ) + occ_level((occ + n_occ - 1 - s) % n_occ)

        def body(t, carry):
            at = pl.ds(pl.multiple_of(t * 64, 64), 64)
            left = level - vcol[pl.ds(pl.multiple_of(y * chunk + t * 64, 64), 64), :]

            def inner(u, carry):
                c = pl.ds(pl.multiple_of(u * LANES, LANES), LANES)
                there = cols(h * half + u * LANES, LANES)
                total = acc[s, at, c]
                for k in range(n_y - 1):
                    total = total + rb[s, k, at, c].astype(jnp.float32)
                divisor = left - vrow[:1, there]
                tt[s, pl.ds(pl.multiple_of(y * chunk + t * 64, 64), 64), there] = (
                    total / divisor
                ).astype(jnp.bfloat16)
                return carry

            return lax.fori_loop(0, half // LANES, inner, carry)

        lax.fori_loop(0, chunk // 64, body, 0)

    def block(s, y_at, which, lo=0, size=None):
        start = pl.multiple_of((y + y_at + n_y) % n_y * chunk + lo, sub)
        return tt.at[s, pl.ds(start, size or chunk), mine if which == 0 else other]

    def across(s):
        part = block(s, 0, 0)
        return send(part, part, ax_s.at[s], ax_r.at[s], partner)

    def along(s, which, way):
        part = block(s, 0, which)
        return send(part, part, a1_s.at[s, which, way], a1_r.at[s, which, way], at_y(1 if way == 0 else n_y - 1))

    def onward(s, which, way):
        part = block(s, -1 if way == 0 else 1, which, 0 if way == 0 else sub, sub)
        return send(part, part, a2_s.at[s, which, way], a2_r.at[s, which, way], at_y(1 if way == 0 else n_y - 1))

    def spread_own(s):
        across(s).start()
        along(s, 0, 0).start()
        along(s, 0, 1).start()

    def spread_partner(s):
        across(s).wait_recv()
        along(s, 1, 0).start()
        along(s, 1, 1).start()

    def forward(s, which):
        for way in (0, 1):
            along(s, which, way).wait_recv()
            onward(s, which, way).start()

    def gathered(s):
        for which in (0, 1):
            for way in (0, 1):
                onward(s, which, way).wait_recv()

    first, second = 1 - core, core

    def wait_factors(s, part):
        @pl.when(s == 1)
        def _():
            ahead_parts[part].wait_recv()

        @pl.when(s == 0)
        def _():
            down_parts[part].wait_recv()

    def relay(part):
        @pl.when(core == 1)
        def _():
            ahead_parts[part].wait_recv()
            up_parts[part].start()

    wait_factors(first, 0)
    wait_factors(first, 1)
    for k in range(n_y):
        if k >= n_y // 2:
            arrived(k)
        partial_integrals(first, own_chunk(k))
        if k == 1:
            relay(0)
    relay(1)
    relay(2)
    finish(first)
    spread_own(first)

    @pl.when(core == 0)
    def _():
        wait_factors(second, 0)
        wait_factors(second, 1)

    def rest(k, carry):
        partial_integrals(second, (y + k) % n_y)
        return carry

    lax.fori_loop(1, n_y + 1, rest, 0)
    spread_partner(first)
    forward(first, 0)
    forward(first, 1)
    finish(second)
    spread_own(second)
    gathered(first)
    wait_factors(first, 2)

    def density(s, t):
        a_rows = pl.ds(pl.multiple_of(t * width, width), width)
        return lax.dot_general(
            jj[s], tt[s, a_rows, :], (((1,), (1,)), ((), ())), preferred_element_type=jnp.float32
        )

    def first_density(t, carry):
        g1[:, pl.ds(pl.multiple_of(t * width, width), width)] = density(first, t)
        return carry

    spread_partner(second)
    forward(second, 0)
    lax.fori_loop(0, virt // width, first_density, 0)
    forward(second, 1)

    @pl.when(core == 0)
    def _():
        wait_factors(second, 2)

    gathered(second)
    per_row = virt // LANES

    def last_density(t, carry):
        total = density(second, t) + g1[:, pl.ds(pl.multiple_of(t * width, width), width)]
        for u in range(width // LANES):
            out_ref[pl.ds(t * (width // LANES) + u, rows, stride=per_row), :] = total[
                :, u * LANES : (u + 1) * LANES
            ]
        return carry

    lax.fori_loop(0, virt // width, last_density, 0)

    for k in range(n_y):
        gather(k, 1 - h).wait_send()
    for part in range(3):
        ahead_parts[part].wait_send()
        down_parts[part].wait_send()
    for s in (0, 1):
        for k in range(n_y - 1):
            send(
                sb.at[s, k], rb.at[s, k], rs_s.at[s, k], rs_r.at[s, k], at_y(1)
            ).wait_send()
        across(s).wait_send()
        for which in (0, 1):
            for way in (0, 1):
                along(s, which, way).wait_send()
                onward(s, which, way).wait_send()


def on_device(factor, occ_energy, vir_energy, occ_pick, vir_pick):
    n_aux, n_occ = lax.axis_size("aux"), lax.axis_size("occ")
    n_y = n_aux // 2
    rows, _, virt = factor.shape
    half, chunk = virt // 2, virt // n_y
    bf16, f32 = jnp.bfloat16, jnp.float32
    dma = pltpu.SemaphoreType.DMA
    vmem = pl.BlockSpec(memory_space=pltpu.VMEM)
    out = pl.pallas_call(
        functools.partial(kernel, n_y, n_occ),
        out_shape=jax.ShapeDtypeStruct((rows * virt // LANES, LANES), f32),
        in_specs=[vmem, vmem, vmem, pl.BlockSpec(memory_space=pltpu.SMEM), vmem],
        out_specs=vmem,
        scratch_shapes=[
            pltpu.VMEM((rows, virt), bf16),
            pltpu.VMEM((virt, 2 * rows), bf16),
            pltpu.VMEM((2, rows, virt), bf16),
            pltpu.VMEM((2, rows, half), bf16),
            pltpu.VMEM((2, n_y - 1, chunk, half), bf16),
            pltpu.VMEM((2, n_y - 1, chunk, half), bf16),
            pltpu.VMEM((2, chunk, half), f32),
            pltpu.VMEM((2, virt, virt), bf16),
            pltpu.VMEM((rows, virt), f32),
            pltpu.VMEM((virt, LANES), f32),
            pltpu.VMEM((8, virt), f32),
            dma((n_y,)), dma((n_y,)),
            dma((3,)), dma((3,)),
            dma((3,)), dma((3,)),
            dma((2, n_y - 1)), dma((2, n_y - 1)),
            dma((2,)), dma((2,)),
            dma((2, 2, 2)), dma((2, 2, 2)),
            dma((2, 2, 2)), dma((2, 2, 2)),
        ],
        compiler_params=pltpu.CompilerParams(
            collective_id=0, has_side_effects=True, vmem_limit_bytes=60 * 2**20
        ),
    )(
        factor.reshape(rows, virt),
        occ_energy.reshape(-1, LANES),
        vir_energy.reshape(-1, LANES),
        occ_pick,
        vir_pick.reshape(-1, LANES),
    )
    return out.reshape(rows, 1, virt)


def solution(mesh):
    placed = (P("aux", "occ", None), P(), P(), P(), P())
    return jax.shard_map(
        on_device, mesh=mesh, in_specs=placed, out_specs=P("aux", "occ", None), check_vma=False
    )
```

time: 428 us -> 285 us (0.67)
  waiting for transfers between devices: 348 us -> 0 us
  Pallas kernels: 0 us -> 277 us
  matrix products: 33.2 us -> 0 us
  local copies, waits for them, and re-layouts: 25.2 us -> 7.76 us
  between operations: 15.9 us -> 0.01 us
    pallas_call x0 -> x1, Pallas kernels: none -> 277 us  [on_device(): pl.pallas_call(functools.partial(kernel, n_y, n_occ), out_shape=jax.Shape...]
    reduce_scatter x2 -> x0, waiting for transfers between devices: 171 us -> none  [pair_density(): lax.psum_scatter(lax.dot_general(right_block, left_block, (((0,), (0,)),...]
    all_gather x2 -> x0, waiting for transfers between devices: 111 us -> none  [pair_density(): lax.all_gather(amplitudes, 'aux', axis=0, tiled=True)]
    ppermute x2 -> x0, waiting for transfers between devices: 65.8 us -> none  [shifted(): return lax.ppermute(block, axis, route)]
    dot_general x4 -> x0, matrix products: 33.2 us -> none  [the longest x2 18.9 us: pair_density(): jnp.dot(right_block, lax.all_gather(amplitudes, 'aux', axis=0, tiled=True...]
    another operation x1 -> x0, local copies, waits for them, and re-layouts: 12.1 us -> none  [on_device(): return jnp.stack(results, axis=1)]
    gather x2 -> x0, local copies, waits for them, and re-layouts: 9.06 us -> none  [the longest x1 8.39 us: on_device(): vir_levels = jnp.take(vir_energy, vir_pick)]
    unnamed x16 -> x1, local copies, waits for them, and re-layouts: 3.39 us -> 7.76 us
  transfers between devices with their start and end apart: 6 -> 0, of which waited for: 6 -> 0; matrix products, arithmetic and copies ran while one was open for 6% -> 0% of each run, Pallas kernels for 0% -> 0%
where the time goes in v1:
time: 285 us
  Pallas kernels  277 us (97%)
  local copies, waits for them, and re-layouts  7.76 us (3%)
    pallas_call x1, Pallas kernels, on_device(): pl.pallas_call(functools.partial(kernel, n_y, n_occ), out_shape=jax.Shape...  277 us
    unnamed x1, local copies, waits for them, and re-layouts  7.76 us

profile of v1, /device:TPU:2, one launch (start us, length us, event | category | flops | bytes accessed | tf_op | source)
XLA Modules:
  0.0 284.8 jit_solution(16343201416196790365)
XLA Ops:
  0.0 277.0 %shard_map.55 = f32[9216,128]{1,0:T(8,128)} custom-call(bf16[768,1536]{1,0:T(8,128)(2,1)} %bitcast.6, f32[8,128]{1,0:T(8,128)} %bitcast.9, f32[24,128]{1,0:T(8,128)} %bitcast.7, s32[32]{0:T(128)} %op_ref.1, s32[12,128]{1,0:T(8,128)} %bitcast.8), custom_call_target="tpu_custom_call" | custom-call | tf_op jit(solution)/shard_map/pallas_call | solution.py:346
  277.0 7.8 %copy.8 = f32[768,1,1536]{2,1,0:T(1,128)} copy(f32[768,1,1536]{2,1,0:T(1,128)} %bitcast.5) | data formatting | bytes 9437184

commit v2 on v1

--- a/solution.py
+++ b/solution.py
@@ -14,7 +14,7 @@
 def kernel(
     n_y, n_occ, f_ref, oe_ref, ve_ref, op_ref, vp_ref, out_ref,
     fx, ft, jj, jx, sb, rb, acc, tt, g1, vcol, vrow,
-    g_s, g_r, z_s, z_r, s_s, s_r, rs_s, rs_r, ax_s, ax_r, a1_s, a1_r, a2_s, a2_r,
+    g_s, g_r, z_s, z_r, w_s, w_r, q_s, q_r, s_s, s_r, rs_s, rs_r, ax_s, ax_r, a1_s, a1_r, a2_s, a2_r,
 ):
     rows, virt = f_ref.shape
     half = virt // 2
@@ -31,6 +31,13 @@
     sibling = {"occ": occ + 1 - 2 * core}
     ahead = {"occ": (occ + 2) % n_occ}
     behind = {"occ": (occ + n_occ - 2) % n_occ}
+    wraps = (occ + 2) % (n_occ // 2) < 2
+    ahead_across = {"aux": (1 - h) * n_y + y, "occ": (occ + 2) % n_occ}
+    facing = {"occ": (occ + n_occ // 2) % n_occ}
+    column = occ // (n_occ // 2) * (n_occ // 2)
+    up_column = {"occ": column + (occ + 2) % (n_occ // 2)}
+    down_column = {"occ": column + (occ + n_occ // 2 - 2) % (n_occ // 2)}
+    behind_across = {"aux": (1 - h) * n_y + y, "occ": (occ + n_occ - 2) % n_occ}
 
     def send(src, dst, s_sem, r_sem, where):
         return pltpu.make_async_remote_copy(
@@ -44,23 +51,75 @@
     mine, other = cols(h * half, half), cols((1 - h) * half, half)
 
     barrier = pltpu.get_barrier_semaphore()
-    peers = [partner, sibling, ahead, behind] + [at_y(k) for k in range(1, n_y)]
+    peers = [partner, sibling, ahead, behind, ahead_across, behind_across]
+    peers = peers + [facing, up_column, down_column] + [at_y(k) for k in range(1, n_y)]
     for peer in peers:
         pl.semaphore_signal(barrier, inc=1, device_id=peer, device_id_type=MESH)
     pl.semaphore_wait(barrier, len(peers))
 
+    def order(k, half_at):
+        per_half = n_y // 2
+        return (half_at + k // per_half) % 2 * per_half + (y + 1 + k) % per_half
+
     def gather(k, half_at):
-        c = cols((half_at * (n_y // 2) + k) % n_y * chunk, chunk)
+        c = cols(order(k, half_at) * chunk, chunk)
         return send(f_ref.at[:, c], fx.at[:, c], g_s.at[k], g_r.at[k], partner)
 
-    for k in range(n_y):
+    for k in range(n_y // 2):
         gather(k, 1 - h).start()
 
+    @pl.when(core == 1)
+    def _():
+        for k in range(n_y // 2, n_y):
+            gather(k, 1 - h).start()
+
+
+    upper, lower = pl.ds(rows // 2, rows // 2), pl.ds(0, rows // 2)
+
+    class Ahead:
+        def __init__(self, part):
+            c = mine if part == 0 else other
+            self.direct = send(f_ref.at[lower, c], jj.at[1, lower, c], z_s.at[part], z_r.at[part], ahead)
+            self.second = send(f_ref.at[upper, c], jj.at[1, upper, c], w_s.at[part], w_r.at[part], ahead)
+            self.detour = send(f_ref.at[upper, c], jj.at[2, upper, c], w_s.at[part], q_r.at[part], facing)
+            self.onward = send(jj.at[2, upper, c], jj.at[1, upper, c], q_s.at[part], w_r.at[part], up_column)
+
+        def start(self):
+            @pl.when(wraps)
+            def _():
+                self.detour.start()
+
+            self.direct.start()
+
+            @pl.when(jnp.logical_not(wraps))
+            def _():
+                self.second.start()
+
+        def hand_on(self):
+            @pl.when(wraps)
+            def _():
+                self.detour.wait_recv()
+                self.onward.start()
+
+        def wait_recv(self):
+            self.direct.wait_recv()
+            self.second.wait_recv()
+
+        def wait_send(self):
+            self.direct.wait_send()
+            self.second.wait_send()
+
+            @pl.when(wraps)
+            def _():
+                self.onward.wait_send()
+
     ahead_parts = (
-        send(f_ref.at[:, mine], jj.at[1, :, mine], z_s.at[0], z_r.at[0], ahead),
+        Ahead(0),
         send(fx.at[:, mine], jx.at[1], z_s.at[1], z_r.at[1], ahead),
-        send(f_ref.at[:, other], jj.at[1, :, other], z_s.at[2], z_r.at[2], ahead),
+        Ahead(2),
     )
+    straight = send(f_ref.at[:, other], jx.at[1], z_s.at[1], z_r.at[1], ahead_across)
+
     down_parts = (
         send(f_ref.at[:, mine], jj.at[0, :, mine], s_s.at[0], s_r.at[0], sibling),
         send(fx.at[:, mine], jx.at[0], s_s.at[1], s_r.at[1], sibling),
@@ -71,7 +130,13 @@
         send(jx.at[1], jx.at[0], s_s.at[1], s_r.at[1], sibling),
         send(jj.at[1, :, other], jj.at[0, :, other], s_s.at[2], s_r.at[2], sibling),
     )
-    ahead_parts[0].start()
+    @pl.when(wraps)
+    def _():
+        straight.start()
+
+    @pl.when(core == 1)
+    def _():
+        ahead_parts[0].start()
 
     @pl.when(core == 0)
     def _():
@@ -86,7 +151,7 @@
         lax.fori_loop(0, chunk // LANES, body, 0)
 
     def turn_own(k, carry):
-        turn(f_ref, (h * (n_y // 2) + k) % n_y, 0)
+        turn(f_ref, order(k, h), 0)
         return carry
 
     lax.fori_loop(0, n_y, turn_own, 0)
@@ -118,7 +183,7 @@
         return jnp.sum(jnp.sum(found, axis=1, keepdims=True), axis=0, keepdims=True)
 
     def own_chunk(k):
-        return (h * (n_y // 2) + k) % n_y
+        return order(k, h)
 
     def arrived(k):
         gather(k, h).wait_recv()
@@ -126,14 +191,22 @@
 
     for k in range(n_y // 2):
         gather(k, h).wait_recv()
-    ahead_parts[1].start()
+
+    @pl.when(jnp.logical_not(wraps))
+    def _():
+        ahead_parts[1].start()
 
     @pl.when(core == 0)
     def _():
         down_parts[1].start()
+        for k in range(n_y // 2, n_y):
+            gather(k, 1 - h).start()
         down_parts[2].start()
 
-    ahead_parts[2].start()
+        @pl.when(jnp.logical_not(wraps))
+        def _():
+            ahead_parts[0].start()
+
     for k in range(n_y // 2):
         turn(fx, own_chunk(k), 1)
 
@@ -238,16 +311,7 @@
             for way in (0, 1):
                 onward(s, which, way).wait_recv()
 
-    first, second = 1 - core, core
-
-    def wait_factors(s, part):
-        @pl.when(s == 1)
-        def _():
-            ahead_parts[part].wait_recv()
-
-        @pl.when(s == 0)
-        def _():
-            down_parts[part].wait_recv()
+    first, second = 0, 1
 
     def relay(part):
         @pl.when(core == 1)
@@ -255,36 +319,68 @@
             ahead_parts[part].wait_recv()
             up_parts[part].start()
 
-    wait_factors(first, 0)
-    wait_factors(first, 1)
-    for k in range(n_y):
-        if k >= n_y // 2:
-            arrived(k)
-        partial_integrals(first, own_chunk(k))
-        if k == 1:
-            relay(0)
+    def given(part):
+        down_parts[part].wait_recv()
+
+    @pl.when(core == 1)
+    def _():
+        given(0)
+        given(1)
+        for k in range(n_y // 2):
+            partial_integrals(first, own_chunk(k))
+        ahead_parts[0].hand_on()
+
+    relay(0)
+    for k in range(n_y // 2, n_y):
+        arrived(k)
+
+        @pl.when(core == 1)
+        def _():
+            partial_integrals(first, own_chunk(k))
+
+    @pl.when((core == 0) & wraps)
+    def _():
+        ahead_parts[0].start()
+
     relay(1)
-    relay(2)
+
+    def chunks(s):
+        def body(k, carry):
+            partial_integrals(s, (y + k) % n_y)
+            return carry
+
+        lax.fori_loop(1, n_y + 1, body, 0)
+
+    @pl.when(core == 0)
+    def _():
+        given(0)
+        given(1)
+        chunks(first)
+        ahead_parts[0].hand_on()
+
+    @pl.when(core == 1)
+    def _():
+        chunks(second)
+
     finish(first)
     spread_own(first)
 
     @pl.when(core == 0)
     def _():
-        wait_factors(second, 0)
-        wait_factors(second, 1)
-
-    def rest(k, carry):
-        partial_integrals(second, (y + k) % n_y)
-        return carry
-
-    lax.fori_loop(1, n_y + 1, rest, 0)
+        ahead_parts[0].wait_recv()
+        ahead_parts[1].wait_recv()
+        chunks(second)
+
+    ahead_parts[2].start()
     spread_partner(first)
     forward(first, 0)
+    ahead_parts[2].hand_on()
     forward(first, 1)
     finish(second)
     spread_own(second)
+    relay(2)
     gathered(first)
-    wait_factors(first, 2)
+    given(2)
 
     def density(s, t):
         a_rows = pl.ds(pl.multiple_of(t * width, width), width)
@@ -303,7 +399,7 @@
 
     @pl.when(core == 0)
     def _():
-        wait_factors(second, 2)
+        ahead_parts[2].wait_recv()
 
     gathered(second)
     per_row = virt // LANES
@@ -351,7 +447,7 @@
         scratch_shapes=[
             pltpu.VMEM((rows, virt), bf16),
             pltpu.VMEM((virt, 2 * rows), bf16),
-            pltpu.VMEM((2, rows, virt), bf16),
+            pltpu.VMEM((3, rows, virt), bf16),
             pltpu.VMEM((2, rows, half), bf16),
             pltpu.VMEM((2, n_y - 1, chunk, half), bf16),
             pltpu.VMEM((2, n_y - 1, chunk, half), bf16),
@@ -361,6 +457,8 @@
             pltpu.VMEM((virt, LANES), f32),
             pltpu.VMEM((8, virt), f32),
             dma((n_y,)), dma((n_y,)),
+            dma((3,)), dma((3,)),
+            dma((3,)), dma((3,)),
             dma((3,)), dma((3,)),
             dma((3,)), dma((3,)),
             dma((2, n_y - 1)), dma((2, n_y - 1)),

time: 285 us -> 228 us (0.80)
  Pallas kernels: 277 us -> 220 us
    pallas_call x1, Pallas kernels: 277 us -> 220 us  [on_device(): pl.pallas_call(functools.partial(kernel, n_y, n_occ), out_shape=jax.Shape...]
where the time goes in v2:
time: 228 us; the launch traced here: 227 us
  Pallas kernels  220 us (96%)
  local copies, waits for them, and re-layouts  7.76 us (3%)
    pallas_call x1, Pallas kernels, on_device(): pl.pallas_call(functools.partial(kernel, n_y, n_occ), out_shape=jax.Shape...  220 us
    unnamed x1, local copies, waits for them, and re-layouts  7.76 us

profile of v2, /device:TPU:2, one launch (start us, length us, event | category | flops | bytes accessed | tf_op | source)
XLA Modules:
  0.0 227.5 jit_solution(2215645161413291734)
XLA Ops:
  0.0 219.7 %shard_map.55 = f32[9216,128]{1,0:T(8,128)} custom-call(bf16[768,1536]{1,0:T(8,128)(2,1)} %bitcast.6, f32[8,128]{1,0:T(8,128)} %bitcast.9, f32[24,128]{1,0:T(8,128)} %bitcast.7, s32[32]{0:T(128)} %op_ref.1, s32[12,128]{1,0:T(8,128)} %bitcast.8), custom_call_target="tpu_custom_call" | custom-call | tf_op jit(solution)/shard_map/pallas_call | solution.py:442
  219.7 7.8 %copy.8 = f32[768,1,1536]{2,1,0:T(1,128)} copy(f32[768,1,1536]{2,1,0:T(1,128)} %bitcast.5) | data formatting | bytes 9437184

commit v3 on v2

--- a/solution.py
+++ b/solution.py
@@ -14,7 +14,7 @@
 def kernel(
     n_y, n_occ, f_ref, oe_ref, ve_ref, op_ref, vp_ref, out_ref,
     fx, ft, jj, jx, sb, rb, acc, tt, g1, vcol, vrow,
-    g_s, g_r, z_s, z_r, w_s, w_r, q_s, q_r, s_s, s_r, rs_s, rs_r, ax_s, ax_r, a1_s, a1_r, a2_s, a2_r,
+    g_s, g_r, z_s, z_r, w_s, w_r, q_s, q_r, s_s, s_r, rs_s, rs_r, ax_s, ax_r, af_s, af_r, a1_s, a1_r, a2_s, a2_r,
 ):
     rows, virt = f_ref.shape
     half = virt // 2
@@ -203,9 +203,11 @@
             gather(k, 1 - h).start()
         down_parts[2].start()
 
-        @pl.when(jnp.logical_not(wraps))
-        def _():
-            ahead_parts[0].start()
+        ahead_parts[0].start()
+
+    @pl.when(core == 1)
+    def _():
+        ahead_parts[0].hand_on()
 
     for k in range(n_y // 2):
         turn(fx, own_chunk(k), 1)
@@ -283,13 +285,17 @@
         part = block(s, 0, 0)
         return send(part, part, ax_s.at[s], ax_r.at[s], partner)
 
+    def across_far(s):
+        part = block(s, 2, 0)
+        return send(part, part, af_s.at[s], af_r.at[s], partner)
+
     def along(s, which, way):
         part = block(s, 0, which)
         return send(part, part, a1_s.at[s, which, way], a1_r.at[s, which, way], at_y(1 if way == 0 else n_y - 1))
 
-    def onward(s, which, way):
-        part = block(s, -1 if way == 0 else 1, which, 0 if way == 0 else sub, sub)
-        return send(part, part, a2_s.at[s, which, way], a2_r.at[s, which, way], at_y(1 if way == 0 else n_y - 1))
+    def onward(s, way):
+        part = block(s, -1 if way == 0 else 1, 0, 0 if way == 0 else sub, sub)
+        return send(part, part, a2_s.at[s, way], a2_r.at[s, way], at_y(1 if way == 0 else n_y - 1))
 
     def spread_own(s):
         across(s).start()
@@ -301,15 +307,20 @@
         along(s, 1, 0).start()
         along(s, 1, 1).start()
 
-    def forward(s, which):
+    def forward(s):
         for way in (0, 1):
-            along(s, which, way).wait_recv()
-            onward(s, which, way).start()
+            along(s, 0, way).wait_recv()
+            onward(s, way).start()
+
+    def spread_far(s):
+        for way in (0, 1):
+            onward(s, way).wait_recv()
+        across_far(s).start()
 
     def gathered(s):
-        for which in (0, 1):
-            for way in (0, 1):
-                onward(s, which, way).wait_recv()
+        for way in (0, 1):
+            along(s, 1, way).wait_recv()
+        across_far(s).wait_recv()
 
     first, second = 0, 1
 
@@ -328,9 +339,7 @@
         given(1)
         for k in range(n_y // 2):
             partial_integrals(first, own_chunk(k))
-        ahead_parts[0].hand_on()
-
-    relay(0)
+
     for k in range(n_y // 2, n_y):
         arrived(k)
 
@@ -338,11 +347,9 @@
         def _():
             partial_integrals(first, own_chunk(k))
 
-    @pl.when((core == 0) & wraps)
-    def _():
-        ahead_parts[0].start()
-
-    relay(1)
+    @pl.when(core == 0)
+    def _():
+        ahead_parts[0].hand_on()
 
     def chunks(s):
         def body(k, carry):
@@ -356,14 +363,15 @@
         given(0)
         given(1)
         chunks(first)
-        ahead_parts[0].hand_on()
-
-    @pl.when(core == 1)
-    def _():
-        chunks(second)
-
+
+    relay(0)
+    relay(1)
     finish(first)
     spread_own(first)
+
+    @pl.when(core == 1)
+    def _():
+        chunks(second)
 
     @pl.when(core == 0)
     def _():
@@ -372,13 +380,15 @@
         chunks(second)
 
     ahead_parts[2].start()
+    forward(first)
     spread_partner(first)
-    forward(first, 0)
     ahead_parts[2].hand_on()
-    forward(first, 1)
     finish(second)
     spread_own(second)
+    spread_far(first)
     relay(2)
+    forward(second)
+    spread_partner(second)
     gathered(first)
     given(2)
 
@@ -392,10 +402,9 @@
         g1[:, pl.ds(pl.multiple_of(t * width, width), width)] = density(first, t)
         return carry
 
-    spread_partner(second)
-    forward(second, 0)
-    lax.fori_loop(0, virt // width, first_density, 0)
-    forward(second, 1)
+    lax.fori_loop(0, virt // (2 * width), first_density, 0)
+    spread_far(second)
+    lax.fori_loop(virt // (2 * width), virt // width, first_density, 0)
 
     @pl.when(core == 0)
     def _():
@@ -425,10 +434,11 @@
                 sb.at[s, k], rb.at[s, k], rs_s.at[s, k], rs_r.at[s, k], at_y(1)
             ).wait_send()
         across(s).wait_send()
-        for which in (0, 1):
-            for way in (0, 1):
-                along(s, which, way).wait_send()
-                onward(s, which, way).wait_send()
+        across_far(s).wait_send()
+        for way in (0, 1):
+            along(s, 0, way).wait_send()
+            along(s, 1, way).wait_send()
+            onward(s, way).wait_send()
 
 
 def on_device(factor, occ_energy, vir_energy, occ_pick, vir_pick):
@@ -463,8 +473,9 @@
             dma((3,)), dma((3,)),
             dma((2, n_y - 1)), dma((2, n_y - 1)),
             dma((2,)), dma((2,)),
+            dma((2,)), dma((2,)),
             dma((2, 2, 2)), dma((2, 2, 2)),
-            dma((2, 2, 2)), dma((2, 2, 2)),
+            dma((2, 2)), dma((2, 2)),
         ],
         compiler_params=pltpu.CompilerParams(
             collective_id=0, has_side_effects=True, vmem_limit_bytes=60 * 2**20

time: 228 us -> 211 us (0.925); the launches traced: 227 us -> 207 us
  Pallas kernels: 220 us -> 200 us
    pallas_call x1, Pallas kernels: 220 us -> 200 us  [on_device(): pl.pallas_call(functools.partial(kernel, n_y, n_occ), out_shape=jax.Shape...]
where the time goes in v3:
time: 211 us; the launch traced here: 207 us
  Pallas kernels  200 us (95%)
  local copies, waits for them, and re-layouts  7.76 us (4%)
    pallas_call x1, Pallas kernels, on_device(): pl.pallas_call(functools.partial(kernel, n_y, n_occ), out_shape=jax.Shape...  200 us
    unnamed x1, local copies, waits for them, and re-layouts  7.76 us

profile of v3, /device:TPU:2, one launch (start us, length us, event | category | flops | bytes accessed | tf_op | source)
XLA Modules:
  0.0 207.3 jit_solution(2645055093072436135)
XLA Ops:
  0.0 199.5 %shard_map.55 = f32[9216,128]{1,0:T(8,128)} custom-call(bf16[768,1536]{1,0:T(8,128)(2,1)} %bitcast.6, f32[8,128]{1,0:T(8,128)} %bitcast.9, f32[24,128]{1,0:T(8,128)} %bitcast.7, s32[32]{0:T(128)} %op_ref.1, s32[12,128]{1,0:T(8,128)} %bitcast.8), custom_call_target="tpu_custom_call" | custom-call | tf_op jit(solution)/shard_map/pallas_call | solution.py:452
  199.5 7.8 %copy.8 = f32[768,1,1536]{2,1,0:T(1,128)} copy(f32[768,1,1536]{2,1,0:T(1,128)} %bitcast.5) | data formatting | bytes 9437184

commit v4 on v3

--- a/solution.py
+++ b/solution.py
@@ -14,7 +14,7 @@
 def kernel(
     n_y, n_occ, f_ref, oe_ref, ve_ref, op_ref, vp_ref, out_ref,
     fx, ft, jj, jx, sb, rb, acc, tt, g1, vcol, vrow,
-    g_s, g_r, z_s, z_r, w_s, w_r, q_s, q_r, s_s, s_r, rs_s, rs_r, ax_s, ax_r, af_s, af_r, a1_s, a1_r, a2_s, a2_r,
+    g_s, g_r, z_s, z_r, w_s, w_r, q_s, q_r, s_s, s_r, rs_s, rs_r, ax_s, ax_r, af_s, af_r, a1_s, a1_r, a2_s, a2_r, turn_sem,
 ):
     rows, virt = f_ref.shape
     half = virt // 2
@@ -199,8 +199,6 @@
     @pl.when(core == 0)
     def _():
         down_parts[1].start()
-        for k in range(n_y // 2, n_y):
-            gather(k, 1 - h).start()
         down_parts[2].start()
 
         ahead_parts[0].start()
@@ -340,8 +338,18 @@
         for k in range(n_y // 2):
             partial_integrals(first, own_chunk(k))
 
+    @pl.when(core == 0)
+    def _():
+        pl.semaphore_wait(turn_sem, 1)
+        for k in range(n_y // 2, n_y):
+            gather(k, 1 - h).start()
+
     for k in range(n_y // 2, n_y):
         arrived(k)
+        if k == n_y - 1:
+            @pl.when(core == 1)
+            def _():
+                pl.semaphore_signal(turn_sem, inc=1, device_id=sibling, device_id_type=MESH)
 
         @pl.when(core == 1)
         def _():
@@ -476,6 +484,7 @@
             dma((2,)), dma((2,)),
             dma((2, 2, 2)), dma((2, 2, 2)),
             dma((2, 2)), dma((2, 2)),
+            pltpu.SemaphoreType.REGULAR,
         ],
         compiler_params=pltpu.CompilerParams(
             collective_id=0, has_side_effects=True, vmem_limit_bytes=60 * 2**20

time: 211 us -> 203 us (0.962)
  the two profiles are of different devices: /device:TPU:2 before, /device:TPU:234 now
where the time goes in v4:
time: 203 us
  Pallas kernels  195 us (96%)
  local copies, waits for them, and re-layouts  7.76 us (4%)
    pallas_call x1, Pallas kernels, on_device(): pl.pallas_call(functools.partial(kernel, n_y, n_occ), out_shape=jax.Shape...  195 us
    unnamed x1, local copies, waits for them, and re-layouts  7.76 us

profile of v4, /device:TPU:234, one launch (start us, length us, event | category | flops | bytes accessed | tf_op | source)
XLA Modules:
  0.0 203.2 jit_solution(16917312108563791372)
XLA Ops:
  0.0 195.5 %shard_map.55 = f32[9216,128]{1,0:T(8,128)} custom-call(bf16[768,1536]{1,0:T(8,128)(2,1)} %bitcast.6, f32[8,128]{1,0:T(8,128)} %bitcast.9, f32[24,128]{1,0:T(8,128)} %bitcast.7, s32[32]{0:T(128)} %op_ref.1, s32[12,128]{1,0:T(8,128)} %bitcast.8), custom_call_target="tpu_custom_call" | custom-call | tf_op jit(solution)/shard_map/pallas_call | solution.py:460
  195.5 7.8 %copy.8 = f32[768,1,1536]{2,1,0:T(1,128)} copy(f32[768,1,1536]{2,1,0:T(1,128)} %bitcast.5) | data formatting | bytes 9437184

commit v5 on v4

--- a/solution.py
+++ b/solution.py
@@ -201,7 +201,9 @@
         down_parts[1].start()
         down_parts[2].start()
 
-        ahead_parts[0].start()
+        @pl.when(jnp.logical_not(wraps))
+        def _():
+            ahead_parts[0].start()
 
     @pl.when(core == 1)
     def _():
@@ -341,6 +343,11 @@
     @pl.when(core == 0)
     def _():
         pl.semaphore_wait(turn_sem, 1)
+
+        @pl.when(wraps)
+        def _():
+            ahead_parts[0].start()
+
         for k in range(n_y // 2, n_y):
             gather(k, 1 - h).start()
 
@@ -388,8 +395,8 @@
         chunks(second)
 
     ahead_parts[2].start()
+    spread_partner(first)
     forward(first)
-    spread_partner(first)
     ahead_parts[2].hand_on()
     finish(second)
     spread_own(second)
@@ -447,6 +454,10 @@
             along(s, 0, way).wait_send()
             along(s, 1, way).wait_send()
             onward(s, way).wait_send()
+
+
+def hand_over(from_ref, to_ref):
+    to_ref[...] = from_ref[...]
 
 
 def on_device(factor, occ_energy, vir_energy, occ_pick, vir_pick):
@@ -496,6 +507,13 @@
         occ_pick,
         vir_pick.reshape(-1, LANES),
     )
+    out = pl.pallas_call(
+        hand_over,
+        out_shape=jax.ShapeDtypeStruct(out.shape, f32),
+        grid=(4,),
+        in_specs=[pl.BlockSpec((out.shape[0] // 4, LANES), lambda i: (i, 0))],
+        out_specs=pl.BlockSpec((out.shape[0] // 4, LANES), lambda i: (i, 0)),
+    )(out)
     return out.reshape(rows, 1, virt)
 
 

time: 203 us -> 197 us (0.970)
  the two profiles are of different devices: /device:TPU:234 before, /device:TPU:2 now
where the time goes in v5:
time: 197 us; the launch traced here: 196 us
  Pallas kernels  196 us (99%)
    pallas_call x1, Pallas kernels, on_device(): pl.pallas_call(functools.partial(kernel, n_y, n_occ), out_shape=jax.Shape...  191 us
    pallas_call x1, Pallas kernels, on_device(): pl.pallas_call(hand_over, out_shape=jax.ShapeDtypeStruct(out.shape, f32),...  5.03 us

profile of v5, /device:TPU:2, one launch (start us, length us, event | category | flops | bytes accessed | tf_op | source)
XLA Modules:
  0.0 196.5 jit_solution(15774930631981382243)
XLA Ops:
  0.0 191.5 %shard_map.55.from_ref = f32[9216,128]{1,0:T(8,128)} custom-call(bf16[768,1536]{1,0:T(8,128)(2,1)} %bitcast.5, f32[8,128]{1,0:T(8,128)} %bitcast.8, f32[24,128]{1,0:T(8,128)} %bitcast.6, s32[32]{0:T(128)} %op_ref.1, s32[12,128]{1,0:T(8,128)} %bitcast.7), custom_call_target="tpu_custom_call" | custom-call | tf_op jit(solution)/shard_map/pallas_call | solution.py:471
  191.5 5.0 %shard_map.56 = f32[9216,128]{1,0:T(8,128)} custom-call(f32[9216,128]{1,0:T(8,128)} %shard_map.55.from_ref), custom_call_target="tpu_custom_call" | custom-call | tf_op jit(solution)/shard_map/pallas_call | solution.py:510

commit v6 on v5

--- a/solution.py
+++ b/solution.py
@@ -417,9 +417,8 @@
         g1[:, pl.ds(pl.multiple_of(t * width, width), width)] = density(first, t)
         return carry
 
-    lax.fori_loop(0, virt // (2 * width), first_density, 0)
     spread_far(second)
-    lax.fori_loop(virt // (2 * width), virt // width, first_density, 0)
+    lax.fori_loop(0, virt // width, first_density, 0)
 
     @pl.when(core == 0)
     def _():

time: 197 us -> 197 us (level)
  no operation moved by 1% of the time
where the time goes in v6:
time: 197 us; the launch traced here: 196 us
  Pallas kernels  196 us (99%)
    pallas_call x1, Pallas kernels, on_device(): pl.pallas_call(functools.partial(kernel, n_y, n_occ), out_shape=jax.Shape...  191 us
    pallas_call x1, Pallas kernels, on_device(): pl.pallas_call(hand_over, out_shape=jax.ShapeDtypeStruct(out.shape, f32),...  5.03 us

profile of v6, /device:TPU:2, one launch (start us, length us, event | category | flops | bytes accessed | tf_op | source)
XLA Modules:
  0.0 196.5 jit_solution(10388477224526087109)
XLA Ops:
  0.0 191.5 %shard_map.55.from_ref = f32[9216,128]{1,0:T(8,128)} custom-call(bf16[768,1536]{1,0:T(8,128)(2,1)} %bitcast.5, f32[8,128]{1,0:T(8,128)} %bitcast.8, f32[24,128]{1,0:T(8,128)} %bitcast.6, s32[32]{0:T(128)} %op_ref.1, s32[12,128]{1,0:T(8,128)} %bitcast.7), custom_call_target="tpu_custom_call" | custom-call | tf_op jit(solution)/shard_map/pallas_call | solution.py:470
  191.5 5.0 %shard_map.56 = f32[9216,128]{1,0:T(8,128)} custom-call(f32[9216,128]{1,0:T(8,128)} %shard_map.55.from_ref), custom_call_target="tpu_custom_call" | custom-call | tf_op jit(solution)/shard_map/pallas_call | solution.py:509
